TPU v7x, 32 devices: a whole 2x2x4 slice. The times are simulated.
32 devices in a mesh: dp: 8 (over z, y), mem: 4 (over x, core).
Axes of the slice: x: 2, y: 2, z: 4, core: 2. Of those that a mesh axis runs over, the one named last changes fastest.
Arguments:
- dec_in: bfloat16 [8, 1024, 1024], P('dp'), may hold values from -6 to 6
- memory: bfloat16 [8, 1024, 1024], P('dp', 'mem'), may hold values from -6 to 6
- dec_len: int32 [8], P('dp'), may hold values from 512 to 1024, as said below
- mem_len: int32 [8], P('dp'), may hold values from 256 to 1024, as said below
- grad_out: bfloat16 [8, 1024, 1024], P('dp'), may hold values from -6 to 6
- self_qkv: bfloat16 [1024, 3072], replicated, may hold values from -0.1875 to 0.1875
- self_out: bfloat16 [1024, 1024], replicated, may hold values from -3 to 3
- cross_q: bfloat16 [1024, 1024], replicated, may hold values from -0.1875 to 0.1875
- cross_kv: bfloat16 [1024, 2048], replicated, may hold values from -0.1875 to 0.1875
- cross_out: bfloat16 [1024, 1024], replicated, may hold values from -3 to 3
- ffn_in: bfloat16 [1024, 4096], replicated, may hold values from -0.1875 to 0.1875
- ffn_out: bfloat16 [4096, 1024], replicated, may hold values from -0.09375 to 0.09375
- proj_bias: float32 [7, 1024], replicated, may hold values from -3 to 3
- ffn_bias: float32 [4096], replicated, may hold values from -3 to 3
- norm_gain: float32 [3, 1024], replicated, may hold values from 0.5 to 1.5
- norm_shift: float32 [3, 1024], replicated, may hold values from -3 to 3
Outputs:
- layer_out: bfloat16 [8, 1024, 1024], P('dp')
- grad_dec: float32 [8, 1024, 1024], P('dp')
- grad_memory: float32 [8, 1024, 1024], P('dp', 'mem')
- grad_self_qkv: float32 [1024, 3072], P('dp')
- grad_self_out: float32 [1024, 1024], P('dp')
- grad_cross_q: float32 [1024, 1024], P('dp')
- grad_cross_kv: float32 [1024, 2048], P('dp')
- grad_cross_out: float32 [1024, 1024], P('dp')
- grad_ffn_in: float32 [1024, 4096], P('dp')
- grad_ffn_out: float32 [4096, 1024], P('dp')
- grad_proj_bias: float32 [7, 1024], replicated
- grad_ffn_bias: float32 [4096], replicated
- grad_norm_gain: float32 [3, 1024], replicated
- grad_norm_shift: float32 [3, 1024], replicated
Inputs may be any that keep to these rules, and one draw needn't show every extreme that they name: `dec_len`: live decoder positions of an item; in every draw some item has all 1024. `mem_len`: valid memory positions of an item, the first ones; in every draw some item has all 1024.
All inputs are finite; a program needn't handle non-finite values.
Results may differ from a plain program's by a relative error of at most 0.023.
Values may be sent and summed in bfloat16 or wider, within the bound.
A program may use at most 448 MiB of HBM per device.

v0:
```python
import jax
import jax.numpy as jnp
from jax import lax
from jax.sharding import PartitionSpec as P

HEAD_DIM = 64
norm_eps = 1e-05
neg_fill = -1e30


def merged(part, axis, combine):
    gathered = jax.tree.map(lambda a: lax.all_gather(a, axis), part)

    def take(source):
        return jax.tree.map(lambda a: lax.dynamic_index_in_dim(a, source, 0, False), gathered)

    return lax.fori_loop(
        1, lax.axis_size(axis), lambda source, state: combine(state, take(source)), take(0)
    )


def product(left_rows, right_rows):
    return jnp.dot(left_rows, right_rows, preferred_element_type=jnp.float32)


def product_tn(left_rows, right_rows):
    return lax.dot_general(
        left_rows, right_rows, (((0,), (0,)), ((), ())), preferred_element_type=jnp.float32
    )


def product_nt(left_rows, right_rows):
    return lax.dot_general(
        left_rows, right_rows, (((1,), (1,)), ((), ())), preferred_element_type=jnp.float32
    )


def split_heads(matrix):
    return matrix.reshape(matrix.shape[0], matrix.shape[1] // HEAD_DIM, HEAD_DIM)


def normalize(hidden, scale_row, shift_row):
    row_mean = jnp.mean(hidden, axis=-1, keepdims=True)
    centered = hidden - row_mean
    variance = jnp.mean(centered * centered, axis=-1, keepdims=True)
    inverse = lax.rsqrt(variance + norm_eps)
    normed = centered * inverse
    return (normed * scale_row + shift_row, normed, inverse)


def norm_back(grad_rows, normed, inverse, scale_row):
    scaled = grad_rows * scale_row
    grad_hidden = inverse * (
        scaled
        - jnp.mean(scaled, axis=-1, keepdims=True)
        - normed * jnp.mean(scaled * normed, axis=-1, keepdims=True)
    )
    return (grad_hidden, jnp.sum(grad_rows * normed, axis=0), jnp.sum(grad_rows, axis=0))


def softmax_rows(scores, allowed, row_max, row_sum):
    masked = jnp.where(allowed, scores, neg_fill)
    return jnp.where(allowed, jnp.exp(masked - row_max), 0.0) / row_sum


def gelu_exact(values):
    return jax.nn.gelu(values, approximate=False)


def merge_stats(first_pair, second_pair):
    larger = jnp.maximum(first_pair[0], second_pair[0])
    return (
        larger,
        first_pair[1] * jnp.exp(first_pair[0] - larger)
        + second_pair[1] * jnp.exp(second_pair[0] - larger),
    )


def column_sum(matrix):
    return jnp.sum(matrix.astype(jnp.float32), axis=0)


def per_device(
    dec_in,
    memory,
    dec_len,
    mem_len,
    grad_out,
    self_qkv,
    self_out,
    cross_q,
    cross_kv,
    cross_out,
    ffn_in,
    ffn_out,
    proj_bias,
    ffn_bias,
    norm_gain,
    norm_shift,
):
    full_rows = dec_in.shape[1]
    model_width = dec_in.shape[2]
    x_rows = dec_in[0]
    mem_rows = memory[0]
    mem_count = mem_rows.shape[0]
    mem_start = lax.axis_index("mem") * mem_count
    zero_bias = jnp.zeros((model_width,), jnp.float32)
    query_pos = jnp.arange(full_rows, dtype=jnp.int32)
    key_pos = jnp.arange(full_rows, dtype=jnp.int32)
    causal = ((key_pos[None, :] <= query_pos[:, None]) & (key_pos[None, :] < dec_len[0]))[None]
    qkv_rows = product(x_rows, self_qkv) + jnp.concatenate([proj_bias[0], zero_bias, proj_bias[1]])
    q_heads = split_heads((qkv_rows[:, :model_width] * 0.125).astype(jnp.bfloat16))
    key_low = qkv_rows[:, model_width : 2 * model_width].astype(jnp.bfloat16)
    value_low = qkv_rows[:, 2 * model_width :].astype(jnp.bfloat16)
    key_all, value_all = (key_low, value_low)
    k_heads = split_heads(key_all)
    v_heads = split_heads(value_all)
    self_scores = jnp.einsum("rhe,che->hrc", q_heads, k_heads, preferred_element_type=jnp.float32)
    self_max = jnp.max(jnp.where(causal, self_scores, neg_fill), axis=-1, keepdims=True)
    self_sum = jnp.sum(
        jnp.where(causal, jnp.exp(jnp.where(causal, self_scores, neg_fill) - self_max), 0.0),
        axis=-1,
        keepdims=True,
    )
    self_weights = softmax_rows(self_scores, causal, self_max, self_sum)
    attended = (
        jnp.einsum(
            "hrc,che->rhe",
            self_weights.astype(jnp.bfloat16),
            v_heads,
            preferred_element_type=jnp.float32,
        )
        .reshape(full_rows, model_width)
        .astype(jnp.bfloat16)
    )
    first_out, first_norm, first_inv = normalize(
        x_rows.astype(jnp.float32) + product(attended, self_out) + proj_bias[2],
        norm_gain[0],
        norm_shift[0],
    )
    first_low = first_out.astype(jnp.bfloat16)
    cq_heads = split_heads(
        ((product(first_low, cross_q) + proj_bias[3]) * 0.125).astype(jnp.bfloat16)
    )
    block_len = mem_rows.shape[0]
    mem_reach = (mem_start + jnp.arange(block_len, dtype=jnp.int32) < mem_len[0])[None, None, :]
    mem_kv = product(mem_rows, cross_kv) + jnp.concatenate([zero_bias, proj_bias[4]])
    kc_heads = split_heads(mem_kv[:, :model_width].astype(jnp.bfloat16))
    vc_heads = split_heads(mem_kv[:, model_width:].astype(jnp.bfloat16))
    cross_scores = jnp.einsum(
        "rhe,che->hrc", cq_heads, kc_heads, preferred_element_type=jnp.float32
    )
    cross_masked = jnp.where(mem_reach, cross_scores, neg_fill)
    local_max = jnp.max(cross_masked, axis=-1)
    local_sum = jnp.sum(
        jnp.where(mem_reach, jnp.exp(cross_masked - local_max[..., None]), 0.0), axis=-1
    )
    cross_max, cross_sum = merged((local_max, local_sum), "mem", merge_stats)
    cross_weights = softmax_rows(
        cross_scores, mem_reach, cross_max[..., None], cross_sum[..., None]
    )
    cross_low = cross_weights.astype(jnp.bfloat16)
    cross_part = jnp.einsum(
        "hrc,che->rhe", cross_low, vc_heads, preferred_element_type=jnp.float32
    ).reshape(full_rows, model_width)
    crossed = lax.psum(cross_part, "mem")
    crossed_low = crossed.astype(jnp.bfloat16)
    second, second_norm, second_inv = normalize(
        first_out + product(crossed_low, cross_out) + proj_bias[5], norm_gain[1], norm_shift[1]
    )
    second_low = second.astype(jnp.bfloat16)
    hidden_pre = product(second_low, ffn_in) + ffn_bias
    activated = gelu_exact(hidden_pre).astype(jnp.bfloat16)
    third_out, third_norm, third_inv = normalize(
        second + product(activated, ffn_out) + proj_bias[6], norm_gain[2], norm_shift[2]
    )
    out_low = third_out.astype(jnp.bfloat16)
    grad_rows_in = grad_out[0]
    cotangent = jnp.where((query_pos < dec_len[0])[:, None], grad_rows_in.astype(jnp.float32), 0.0)
    grad_third, gain_three, shift_three = norm_back(cotangent, third_norm, third_inv, norm_gain[2])
    ffn_grad = grad_third.astype(jnp.bfloat16)
    grad_hidden = product_nt(ffn_grad, ffn_out)
    hidden_grad = jax.vjp(gelu_exact, hidden_pre)[1](grad_hidden)[0].astype(jnp.bfloat16)
    grad_second, gain_two, shift_two = norm_back(
        grad_third + product_nt(hidden_grad, ffn_in), second_norm, second_inv, norm_gain[1]
    )
    cross_grad = grad_second.astype(jnp.bfloat16)
    crossed_grad = split_heads(product_nt(cross_grad, cross_out).astype(jnp.bfloat16))
    grad_vc = jnp.einsum(
        "hrc,rhe->che", cross_low, crossed_grad, preferred_element_type=jnp.float32
    ).reshape(block_len, model_width)
    grad_cw = jnp.einsum("rhe,che->hrc", crossed_grad, vc_heads, preferred_element_type=jnp.float32)
    delta_part = jnp.sum(cross_weights * grad_cw, axis=-1)
    cross_delta = lax.psum(delta_part, "mem")
    cross_ds = (cross_weights * (grad_cw - cross_delta[..., None])).astype(jnp.bfloat16)
    cq_part = jnp.einsum(
        "hrc,che->rhe", cross_ds, kc_heads, preferred_element_type=jnp.float32
    ).reshape(full_rows, model_width)
    cq_total = lax.psum(cq_part, "mem")
    cq_grad = (cq_total * 0.125).astype(jnp.bfloat16)
    grad_kc = jnp.einsum(
        "hrc,rhe->che", cross_ds, cq_heads, preferred_element_type=jnp.float32
    ).reshape(block_len, model_width)
    kv_full = jnp.concatenate([grad_kc, grad_vc], axis=1)
    own_kv = kv_full.astype(jnp.bfloat16)
    grad_memory = product_nt(own_kv, cross_kv)[None]
    grad_first, gain_one, shift_one = norm_back(
        grad_second + product_nt(cq_grad, cross_q), first_norm, first_inv, norm_gain[0]
    )
    self_grad = grad_first.astype(jnp.bfloat16)
    attended_grad = split_heads(product_nt(self_grad, self_out).astype(jnp.bfloat16))
    scores_again = jnp.einsum("rhe,che->hrc", q_heads, k_heads, preferred_element_type=jnp.float32)
    weights_again = softmax_rows(scores_again, causal, self_max, self_sum)
    grad_v = jnp.einsum(
        "hrc,rhe->che",
        weights_again.astype(jnp.bfloat16),
        attended_grad,
        preferred_element_type=jnp.float32,
    ).reshape(full_rows, model_width)
    grad_sw = jnp.einsum("rhe,che->hrc", attended_grad, v_heads, preferred_element_type=jnp.float32)
    self_ds = (
        weights_again * (grad_sw - jnp.sum(weights_again * grad_sw, axis=-1, keepdims=True))
    ).astype(jnp.bfloat16)
    grad_q = (
        jnp.einsum("hrc,che->rhe", self_ds, k_heads, preferred_element_type=jnp.float32).reshape(
            full_rows, model_width
        )
        * 0.125
    )
    grad_k = jnp.einsum(
        "hrc,rhe->che", self_ds, q_heads, preferred_element_type=jnp.float32
    ).reshape(full_rows, model_width)
    grad_k_own, grad_v_own = (grad_k, grad_v)
    qkv_grad = jnp.concatenate([grad_q, grad_k_own, grad_v_own], axis=1).astype(jnp.bfloat16)
    grad_dec_rows = grad_first + product_nt(qkv_grad, self_qkv)
    layer_out = out_low[None]
    grad_dec = grad_dec_rows[None]
    qkv_weight_grad = product_tn(x_rows, qkv_grad)
    self_out_grad = product_tn(attended, self_grad)
    cross_q_grad = product_tn(first_low, cq_grad)
    cross_kv_grad = product_tn(mem_rows, own_kv)
    cross_out_grad = product_tn(crossed_low, cross_grad)
    ffn_in_grad = product_tn(second_low, hidden_grad)
    ffn_out_grad = product_tn(activated, ffn_grad)
    qkv_sums = column_sum(qkv_grad)
    bias_rest = jnp.stack(
        [
            qkv_sums[:model_width],
            qkv_sums[2 * model_width :],
            column_sum(self_grad),
            column_sum(cq_grad),
            column_sum(cross_grad),
            column_sum(ffn_grad),
        ]
    )
    value_bias = column_sum(own_kv[:, model_width:])
    ffn_bias_grad = column_sum(hidden_grad)
    gain_rows = jnp.stack([gain_one, gain_two, gain_three])
    shift_rows = jnp.stack([shift_one, shift_two, shift_three])
    matrices = (
        lax.psum_scatter(qkv_weight_grad, "dp", scatter_dimension=0, tiled=True),
        lax.psum_scatter(self_out_grad, "dp", scatter_dimension=0, tiled=True),
        lax.psum_scatter(cross_q_grad, "dp", scatter_dimension=0, tiled=True),
        lax.psum_scatter(cross_kv_grad, "dp", scatter_dimension=0, tiled=True),
        lax.psum_scatter(cross_out_grad, "dp", scatter_dimension=0, tiled=True),
        lax.psum_scatter(ffn_in_grad, "dp", scatter_dimension=0, tiled=True),
        lax.psum_scatter(ffn_out_grad, "dp", scatter_dimension=0, tiled=True),
    )
    vectors = lax.psum((bias_rest, ffn_bias_grad, gain_rows, shift_rows, value_bias), "dp")
    kv_total, value_total = (
        lax.psum(matrices[3].astype(jnp.bfloat16), "mem").astype(jnp.float32),
        lax.psum(vectors[4].astype(jnp.bfloat16), "mem").astype(jnp.float32),
    )
    matrices = (
        matrices[0],
        matrices[1],
        matrices[2],
        kv_total,
        matrices[4],
        matrices[5],
        matrices[6],
    )
    vectors = (vectors[0], vectors[1], vectors[2], vectors[3], value_total)
    bias_grad = jnp.concatenate([vectors[0][:4], vectors[4][None], vectors[0][4:]], axis=0)
    return (
        layer_out,
        grad_dec,
        grad_memory,
        matrices[0],
        matrices[1],
        matrices[2],
        matrices[3],
        matrices[4],
        matrices[5],
        matrices[6],
        bias_grad,
        vectors[1],
        vectors[2],
        vectors[3],
    )


def solution(mesh):
    in_specs = (
        P("dp", None, None),
        P("dp", "mem", None),
        P("dp"),
        P("dp"),
        P("dp", None, None),
        P(),
        P(),
        P(),
        P(),
        P(),
        P(),
        P(),
        P(),
        P(),
        P(),
        P(),
    )
    out_specs = (
        P("dp", None, None),
        P("dp", None, None),
        P("dp", "mem", None),
        P("dp", None),
        P("dp", None),
        P("dp", None),
        P("dp", None),
        P("dp", None),
        P("dp", None),
        P("dp", None),
        P(),
        P(),
        P(),
        P(),
    )
    return jax.shard_map(
        per_device, mesh=mesh, in_specs=in_specs, out_specs=out_specs, check_vma=False
    )
```

profile of v0, /device:TPU:0, one launch (start us, length us, event | category | flops | bytes accessed | tf_op | source)
XLA Modules:
  0.0 1810.6 jit_solution(15955320089730400923)
XLA Ops:
  27.2 12.1 fusion.80
  57.7 35.8 %fusion.81 = (f32[16,1024]{1,0:T(8,128)S(1)}, f32[16,1024,1024]{1,2,0:T(8,128)}) fusion(pred[1024,1024]{0,1:T(8,128)(4,1)S(1)} %fusion.35, bf16[1024,16,64]{0,2,1:T(8,128)(2,1)} %bitcast.166, bf16[1024,16,64]{0,2,1:T(8,128)(2,1)} %bitcast.171), kind=kOutput, calls=%fused_computation.155 | convolution fusion | flops 2214593536 | bytes 72417280 | tf_op jit(solution)/shard_map/sub | solution.py:63
  93.5 24.3 %fusion.42 = bf16[16,64,1024]{2,1,0:T(8,128)(2,1)} fusion(bf16[1024,16,64]{0,2,1:T(8,128)(2,1)} %bitcast.181, f32[16,1024,1024]{1,2,0:T(8,128)} %get-tuple-element.239, f32[16,1024]{1,0:T(8,128)S(1)} %get-tuple-element.238), kind=kOutput, calls=%fused_computation.103 | convolution fusion | flops 2182086656 | bytes 71368704 | tf_op jit(solution)/shard_map/hrc,che->rhe/dot_general | solution.py:127
  117.9 4.3 fusion.82
  132.1 8.9 select_reduce_fusion.2
  141.0 7.2 all-gather
  148.2 9.6 select_reduce_fusion.1
  157.8 5.9 all-gather.1
  163.9 10.4 fusion.33
  174.4 77.8 %all-reduce.13 = bf16[1024,1024]{0,1:T(8,128)(2,1)} all-reduce(f32[1024,1024]{0,1:T(8,128)} %bitcast.178), channel_id=1, replica_groups=mesh['dp'=8,'mem'=4] {'mem'}, use_global_device_ids=true, to_apply=%region_8.9 | all-reduce | flops 1048576 | bytes 6291456 | tf_op jit(solution)/shard_map/psum | solution.py:166
  252.2 6.5 fusion.83
  260.7 47.8 %multiply_convert_fusion.2 = (bf16[1024,4096]{1,0:T(8,128)(2,1)}, f32[1024,4096]{1,0:T(8,128)}, f32[1024,4096]{1,0:T(8,128)}) fusion(f32[4096]{0:T(1024)S(1)} %copy-done.76, bf16[1024,4096]{1,0:T(8,128)(2,1)} %param.28, bf16[1024,1024]{0,1:T(8,128)(2,1)S(1)} %fusion.69.clone.4), kind=kOutput, calls=%fused_computation.20 | convolution fusion | flops 8866758656 | bytes 52445184 | tf_op jit(solution)/shard_map/dot_general | solution.py:23
  308.5 16.8 fusion.84
  331.8 4.3 convert_reduce_fusion.2
  336.0 24.5 %convert_reduce_fusion = (f32[4096]{0:T(1024)}, bf16[1024,4096]{1,0:T(8,128)(2,1)}) fusion(f32[1024,4096]{1,0:T(8,128)} %get-tuple-element.215, f32[1024,4096]{1,0:T(8,128)} %get-tuple-element.246, f32[4096]{0:T(1024)S(1)} %copy-done.76, bf16[1024,1024]{0,1:T(8,128)(2,1)} %get-tuple-element.209, bf16[4096,1024]{1,0:T(8,128)(2,1)} %param.29), kind=kOutput, calls=%fused_computation.16 | convolution fusion | flops 8661233664 | bytes 52461568 | tf_op jit(solution)/shard_map/dot_general | solution.py:33
  360.5 18.5 %multiply_reduce_fusion.2 = (f32[1024]{0:T(1024)}, f32[1024]{0:T(1024)S(1)}, f32[1024]{0:T(1024)S(1)}, f32[1024]{0:T(1024)}, f32[1024,1024]{0,1:T(8,128)S(1)}) fusion(f32[1024,1024]{0,1:T(8,128)S(1)} %copy-done.4, f32[1024]{0:T(1024)S(1)} %add_rsqrt_fusion.1, f32[1024]{0:T(1024)S(1)} %broadcast_multiply_fusion.7, f32[1024]{0:T(1024)S(1)} %bitcast.194, ...), kind=kOutput, calls=%fused_computation.60 | convolution fusion | flops 8609853440 | bytes 31507456 | tf_op jit(solution)/shard_map/dot_general | solution.py:33
  383.5 14.6 multiply_reduce_fusion.1
  398.1 31.9 %all-reduce.8.cloned.1.call-done = f32[16,1024]{1,0:T(8,128)} async-done(((f32[16,1024]{1,0:T(8,128)}), f32[16,1024]{1,0:T(8,128)}) %all-reduce.8.cloned.1.call-update) | async-done | bytes 65552 | tf_op jit(solution)/shard_map/psum | solution.py:194
  430.0 12.4 multiply_convert_fusion.1
  446.8 5.3 copy.76
  452.3 9.6 fusion.48
  461.9 6.3 convolution_convert_fusion.3
  469.1 4.5 convolution_bitcast_fusion.1
  473.6 64.2 %all-reduce.10.cloned.1.call-done = f32[1024,1024]{1,0:T(8,128)} async-done(((f32[1024,1024]{1,0:T(8,128)}), f32[1024,1024]{1,0:T(8,128)}) %all-reduce.10.cloned.1.call-update) | async-done | bytes 4194320 | tf_op jit(solution)/shard_map/psum | solution.py:199
  537.9 8.5 multiply_reduce_fusion.3
  551.6 43.5 %multiply_reduce_fusion = (f32[16,1024]{1,0:T(8,128)S(1)}, f32[16,1024,1024]{1,2,0:T(8,128)}) fusion(f32[16,1024,1024]{1,2,0:T(8,128)} %get-tuple-element.239, f32[16,1024]{1,0:T(8,128)S(1)} %copy-done.33, bf16[1024,16,64]{0,2,1:T(8,128)(2,1)S(1)} %bitcast.235, bf16[1024,16,64]{0,2,1:T(8,128)(2,1)S(1)} %bitcast.182), kind=kOutput, calls=%fused_computation.7 | convolution fusion | flops 2197798912 | bytes 138543104 | tf_op jit(solution)/shard_map/rhe,che->hrc/dot_general | solution.py:220
  595.1 54.7 %multiply_convert_fusion = bf16[16,1024,1024]{1,2,0:T(8,128)(2,1)} fusion(f32[16,1024,1024]{1,2,0:T(8,128)} %get-tuple-element.254, f32[16,1024]{1,0:T(8,128)S(1)} %get-tuple-element.253, f32[16,1024,1024]{1,2,0:T(8,128)} %get-tuple-element.239, f32[16,1024]{1,0:T(8,128)S(1)} %copy-done.33), kind=kLoop, calls=%fused_computation.6 | loop fusion | flops 67108864 | bytes 167903232 | tf_op jit(solution)/shard_map/convert_element_type | solution.py:223
  649.8 17.3 convolution_convert_fusion
  667.2 18.7 %multiply_convert_fusion.3 = bf16[16,64,1024]{2,1,0:T(8,128)(2,1)} fusion(bf16[1024,16,64]{0,2,1:T(8,128)(2,1)} %bitcast.172, bf16[16,1024,1024]{1,2,0:T(8,128)(2,1)} %multiply_convert_fusion), kind=kOutput, calls=%fused_computation.67 | convolution fusion | flops 2149580800 | bytes 37748736 | tf_op jit(solution)/shard_map/hrc,che->rhe/dot_general | solution.py:225
  685.9 25.3 %fusion.45 = bf16[16,64,1024]{2,1,0:T(8,128)(2,1)} fusion(bf16[1024,16,64]{0,2,1:T(8,128)(2,1)} %bitcast.236, f32[16,1024,1024]{1,2,0:T(8,128)} %get-tuple-element.239, f32[16,1024]{1,0:T(8,128)S(1)} %copy-done.33), kind=kOutput, calls=%fused_computation.104 | convolution fusion | flops 2182086656 | bytes 71368704 | tf_op jit(solution)/shard_map/hrc,rhe->che/dot_general | solution.py:214
  713.3 13.7 convolution_bitcast_fusion
  727.3 7.3 fusion.51
  735.3 7.9 fusion.65
  743.3 7.1 fusion.59
  751.1 16.6 fusion.66
  768.1 16.3 fusion.86
  789.6 4.6 convolution_bitcast_fusion.2
  794.4 4.6 convert_reduce_fusion.1
  799.5 41.7 %all-reduce.14 = (f32[6,1024]{1,0:T(8,128)S(1)}, bf16[1024]{0:T(1024)(128)(2,1)S(1)}, f32[4096]{0:T(1024)}, f32[3,1024]{1,0:T(4,128)}, f32[3,1024]{1,0:T(4,128)}) all-reduce(f32[6,1024]{1,0:T(8,128)S(1)} %stack.51, f32[1024]{0:T(1024)S(1)} %convert_reduce_fusion.6, f32[4096]{0:T(1024)S(1)} %copy-done.58, ...), channel_id=1, replica_groups=mesh['dp'=8,'mem'=4] {'dp'}, use_global_device_ids=true, to_apply=%region_36.37 | all-reduce | flops 17408 | bytes 137216 | tf_op jit(solution)/shard_map/psum | solution.py:269
  841.2 12.4 add_bitcast_fusion
  853.6 5.5 copy.85
  859.2 6.1 psum.76
  868.1 91.6 %reduce-scatter.8.cloned.1.call-done = f32[128,3072]{0,1:T(8,128)} async-done(((f32[1024,3072]{0,1:T(8,128)}), f32[128,3072]{0,1:T(8,128)}) %reduce-scatter.8.cloned.1.call-update) | async-done | bytes 1572880 | tf_op jit(solution)/shard_map/reduce_scatter | solution.py:261
  962.7 88.5 %reduce-scatter.16.cloned.1.call-done = f32[128,1024]{1,0:T(8,128)} async-done(((f32[1024,1024]{1,0:T(8,128)}), f32[128,1024]{1,0:T(8,128)}) %reduce-scatter.16.cloned.1.call-update) | async-done | bytes 524304 | tf_op jit(solution)/shard_map/reduce_scatter | solution.py:265
  1051.2 92.2 %reduce-scatter.12.cloned.1.call-done = f32[128,1024]{1,0:T(8,128)} async-done(((f32[1024,1024]{1,0:T(8,128)}), f32[128,1024]{1,0:T(8,128)}) %reduce-scatter.12.cloned.1.call-update) | async-done | bytes 524304 | tf_op jit(solution)/shard_map/reduce_scatter | solution.py:263
  1143.4 92.2 %reduce-scatter.10.cloned.1.call-done = f32[128,1024]{1,0:T(8,128)} async-done(((f32[1024,1024]{1,0:T(8,128)}), f32[128,1024]{1,0:T(8,128)}) %reduce-scatter.10.cloned.1.call-update) | async-done | bytes 524304 | tf_op jit(solution)/shard_map/reduce_scatter | solution.py:262
  1235.6 284.2 %reduce-scatter.18.cloned.1.call-done = f32[128,4096]{1,0:T(8,128)} async-done(((f32[1024,4096]{1,0:T(8,128)}), f32[128,4096]{1,0:T(8,128)}) %reduce-scatter.18.cloned.1.call-update) | async-done | bytes 2097168 | tf_op jit(solution)/shard_map/reduce_scatter | solution.py:266
  1519.8 283.5 %reduce-scatter.20.cloned.1.call-done = f32[512,1024]{1,0:T(8,128)} async-done(((f32[4096,1024]{1,0:T(8,128)}), f32[512,1024]{1,0:T(8,128)}) %reduce-scatter.20.cloned.1.call-update) | async-done | bytes 2097168 | tf_op jit(solution)/shard_map/reduce_scatter | solution.py:267
  (244 shorter events, 86.5 us)
Async XLA Ops:
  7.2 116.9 %copy-start = (bf16[1024,1024]{1,0:T(8,128)(2,1)S(1)}, bf16[1024,1024]{1,0:T(8,128)(2,1)}, u32[]{:S(2)}) copy-start(bf16[1024,1024]{1,0:T(8,128)(2,1)} %param.25) | copy-start | bytes 6291460
  7.2 422.8 %all-reduce.8.cloned.1.call-start = ((), (), s32[]{:S(2)}) async-start(), calls=%async_computation.7 | async-start | bytes 131072 | tf_op jit(solution)/shard_map/psum | solution.py:194
  8.7 10.3 copy-start.59
  93.5 24.3 %copy-start.32 = (f32[16,1024]{1,0:T(8,128)}, f32[16,1024]{1,0:T(8,128)S(1)}, u32[]{:S(2)}) copy-start(f32[16,1024]{1,0:T(8,128)S(1)} %get-tuple-element.238) | copy-start | bytes 196612
  93.5 24.3 %copy-start.26 = (bf16[1,1024,1024]{1,2,0:T(8,128)(2,1)S(1)}, bf16[1,1024,1024]{1,2,0:T(8,128)(2,1)}, u32[]{:S(2)}) copy-start(bf16[1,1024,1024]{1,2,0:T(8,128)(2,1)} %copy.62) | copy-start | bytes 6291460
  93.5 24.3 %copy-start.66 = (f32[1,1024]{1,0:T(1,128)S(1)}, f32[1,1024]{1,0:T(1,128)}, u32[]{:S(2)}) copy-start(f32[1,1024]{1,0:T(1,128)} %get-tuple-element.224) | copy-start | bytes 12292
  93.5 24.3 %copy-start.74 = (bf16[1024,1024]{1,0:T(8,128)(2,1)S(1)}, bf16[1024,1024]{1,0:T(8,128)(2,1)}, u32[]{:S(2)}) copy-start(bf16[1024,1024]{1,0:T(8,128)(2,1)} %param.24) | copy-start | bytes 6291460
  122.2 129.9 %copy-start.41 = (f32[1024]{0:T(1024)}, f32[1024]{0:T(1024)S(1)}, u32[]{:S(2)}) copy-start(f32[1024]{0:T(1024)S(1)} %broadcast_multiply_fusion.8) | copy-start | bytes 12292
  122.7 129.4 %copy-start.49 = (f32[1024]{0:T(1024)}, f32[1024]{0:T(1024)S(1)}, u32[]{:S(2)}) copy-start(f32[1024]{0:T(1024)S(1)} %add_rsqrt_fusion.2) | copy-start | bytes 12292
  132.1 31.8 %copy-start.61 = (pred[256]{0:T(512)(128)(4,1)}, pred[256]{0:T(512)(128)(4,1)S(1)}, u32[]{:S(2)}) copy-start(pred[256]{0:T(512)(128)(4,1)S(1)} %add_compare_fusion) | copy-start | bytes 772
  148.2 15.7 copy-start.30
  163.9 10.5 copy-start.18
  163.9 10.5 copy-start.20
  174.4 77.8 %copy-start.64 = (f32[1,1024]{1,0:T(1,128)S(1)}, f32[1,1024]{1,0:T(1,128)}, u32[]{:S(2)}) copy-start(f32[1,1024]{1,0:T(1,128)} %get-tuple-element.227) | copy-start | bytes 12292
  258.7 120.2 %copy-start.34 = (f32[1024]{0:T(1024)}, f32[1024]{0:T(1024)S(1)}, u32[]{:S(2)}) copy-start(f32[1024]{0:T(1024)S(1)} %broadcast_multiply_fusion.7) | copy-start | bytes 12292
  259.2 119.7 %copy-start.36 = (f32[1024]{0:T(1024)}, f32[1024]{0:T(1024)S(1)}, u32[]{:S(2)}) copy-start(f32[1024]{0:T(1024)S(1)} %add_rsqrt_fusion.1) | copy-start | bytes 12292
  260.7 47.8 %copy-start.63 = (f32[1,1024]{1,0:T(1,128)S(1)}, f32[1,1024]{1,0:T(1,128)}, u32[]{:S(2)}) copy-start(f32[1,1024]{1,0:T(1,128)} %get-tuple-element.221) | copy-start | bytes 12292
  308.5 19.7 %copy-start.6 = (bf16[1,1024,1024]{1,2,0:T(8,128)(2,1)S(1)}, bf16[1,1024,1024]{1,2,0:T(8,128)(2,1)}, u32[]{:S(2)}) copy-start(bf16[1,1024,1024]{1,2,0:T(8,128)(2,1)} %copy.73) | copy-start | bytes 6291460
  336.0 24.5 %copy-start.4 = (f32[1024,1024]{0,1:T(8,128)S(1)}, f32[1024,1024]{0,1:T(8,128)}, u32[]{:S(2)}) copy-start(f32[1024,1024]{0,1:T(8,128)} %copy-done.3) | copy-start | bytes 12582916
  383.4 14.6 copy-start.77
  398.1 139.8 %all-reduce.10.cloned.1.call-start = ((), (), s32[]{:S(2)}) async-start(), calls=%async_computation.8 | async-start | bytes 8388608 | tf_op jit(solution)/shard_map/psum | solution.py:199
  430.0 12.4 copy-start.14
  452.2 259.0 %reduce-scatter.14.cloned.1.call-start = ((), (), s32[]{:S(2)}) async-start(), calls=%async_computation.12 | async-start | bytes 9437184 | tf_op jit(solution)/shard_map/reduce_scatter | solution.py:264
  452.3 9.6 copy-start.7
  461.9 6.4 copy-start.22
  461.9 7.1 copy-start.29
  473.5 64.3 %copy-start.42 = (f32[1024]{0:T(1024)S(1)}, f32[1024]{0:T(1024)}, u32[]{:S(2)}) copy-start(f32[1024]{0:T(1024)} %copy-done.41) | copy-start | bytes 12292
  473.6 64.3 %copy-start.50 = (f32[1024]{0:T(1024)S(1)}, f32[1024]{0:T(1024)}, u32[]{:S(2)}) copy-start(f32[1024]{0:T(1024)} %copy-done.49) | copy-start | bytes 12292
  473.6 64.3 %copy-start.55 = (f32[1,1024]{1,0:T(1,128)S(1)}, f32[1,1024]{1,0:T(1,128)}, u32[]{:S(2)}) copy-start(f32[1,1024]{1,0:T(1,128)} %get-tuple-element.229) | copy-start | bytes 12292
  473.6 392.3 %all-reduce.12.cloned.1.call-start = ((), (), s32[]{:S(2)}) async-start(), calls=%async_computation.13 | async-start | bytes 1048576 | tf_op jit(solution)/shard_map/psum | solution.py:271
  537.9 8.5 copy-start.9
  550.8 44.3 %copy-start.78 = (bf16[1024,1024]{0,1:T(8,128)(2,1)}, bf16[1024,1024]{0,1:T(8,128)(2,1)S(1)}, u32[]{:S(2)}) copy-start(bf16[1024,1024]{0,1:T(8,128)(2,1)S(1)} %convolution_convert_fusion.1) | copy-start | bytes 6291460
  595.1 54.7 %copy-start.10 = (bf16[1024,1024]{0,1:T(8,128)(2,1)S(1)}, bf16[1024,1024]{0,1:T(8,128)(2,1)}, u32[]{:S(2)}) copy-start(bf16[1024,1024]{0,1:T(8,128)(2,1)} %copy.64) | copy-start | bytes 6291460
  685.9 27.4 %copy-start.11 = (bf16[16,64,1024]{2,1,0:T(8,128)(2,1)S(1)}, bf16[16,64,1024]{2,1,0:T(8,128)(2,1)}, u32[]{:S(2)}) copy-start(bf16[16,64,1024]{2,1,0:T(8,128)(2,1)} %convolution_convert_fusion) | copy-start | bytes 6291460
  713.3 246.4 %reduce-scatter.8.cloned.1.call-start = ((), (), s32[]{:S(2)}) async-start(), calls=%async_computation.9 | async-start | bytes 14155776 | tf_op jit(solution)/shard_map/reduce_scatter | solution.py:261
  727.0 324.2 %reduce-scatter.16.cloned.1.call-start = ((), (), s32[]{:S(2)}) async-start(), calls=%async_computation.14 | async-start | bytes 4718592 | tf_op jit(solution)/shard_map/reduce_scatter | solution.py:265
  734.6 408.8 %reduce-scatter.12.cloned.1.call-start = ((), (), s32[]{:S(2)}) async-start(), calls=%async_computation.11 | async-start | bytes 4718592 | tf_op jit(solution)/shard_map/reduce_scatter | solution.py:263
  743.3 492.4 %reduce-scatter.10.cloned.1.call-start = ((), (), s32[]{:S(2)}) async-start(), calls=%async_computation.10 | async-start | bytes 4718592 | tf_op jit(solution)/shard_map/reduce_scatter | solution.py:262
  750.5 769.3 %reduce-scatter.18.cloned.1.call-start = ((), (), s32[]{:S(2)}) async-start(), calls=%async_computation.15 | async-start | bytes 18874368 | tf_op jit(solution)/shard_map/reduce_scatter | solution.py:266
  767.8 1035.5 %reduce-scatter.20.cloned.1.call-start = ((), (), s32[]{:S(2)}) async-start(), calls=%async_computation.16 | async-start | bytes 18874368 | tf_op jit(solution)/shard_map/reduce_scatter | solution.py:267
  794.3 5.1 copy-start.48
  794.3 5.1 copy-start.68
  794.3 5.1 copy-start.70
  794.3 5.1 copy-start.47
  794.3 5.1 copy-start.67
  794.3 5.1 copy-start.69
  794.3 5.1 copy-start.58
  853.6 949.7 %copy-start.1 = (bf16[1024,1024]{1,0:T(8,128)(2,1)S(1)}, bf16[1024,1024]{1,0:T(8,128)(2,1)}, u32[]{:S(2)}) copy-start(bf16[1024,1024]{1,0:T(8,128)(2,1)} %param.25) | copy-start | bytes 6291460
  (41 other events, 100.6 us)
Sparse Core Ops, SparseCore 0:
  398.2 31.7 all-reduce.7
  452.3 85.4 all-reduce.9
  541.5 147.9 reduce-scatter.13
  713.4 33.2 all-reduce.11
  750.1 209.5 reduce-scatter.7
  963.8 87.3 reduce-scatter.15
  1055.4 87.9 reduce-scatter.11
  1147.6 87.9 reduce-scatter.9
  1240.0 279.7 reduce-scatter.17
  1524.0 279.2 reduce-scatter.19
where the time goes:
time: 1820 us; the launch traced here: 1810 us
  waiting for transfers between devices  1030 us (57%)
  matrix products  461 us (25%)
  blocking collectives  139 us (8%)
  other arithmetic  105 us (6%)
  local copies, waits for them, and re-layouts  60.3 us (3%)
    reduce_scatter x1, waiting for transfers between devices, per_device(): lax.psum_scatter(ffn_in_grad, 'dp', scatter_dimension=0, tiled=True)  284 us
    reduce_scatter x1, waiting for transfers between devices, per_device(): lax.psum_scatter(ffn_out_grad, 'dp', scatter_dimension=0, tiled=True)  284 us
    dot_general x7, matrix products, product(): return jnp.dot(left_rows, right_rows, preferred_element_type=jnp.float32)  95.2 us
    reduce_scatter x1, waiting for transfers between devices, per_device(): lax.psum_scatter(self_out_grad, 'dp', scatter_dimension=0, tiled=True)  92.2 us
    reduce_scatter x1, waiting for transfers between devices, per_device(): lax.psum_scatter(cross_q_grad, 'dp', scatter_dimension=0, tiled=True)  92.2 us
    reduce_scatter x1, waiting for transfers between devices, per_device(): lax.psum_scatter(qkv_weight_grad, 'dp', scatter_dimension=0, tiled=True)  91.6 us
    reduce_scatter x1, waiting for transfers between devices, per_device(): lax.psum_scatter(cross_out_grad, 'dp', scatter_dimension=0, tiled=True)  88.5 us
    psum x1, blocking collectives, per_device(): crossed = lax.psum(cross_part, 'mem')  77.8 us
  transfers between devices with their start and end apart: 10, of which 8 were waited for; matrix products, arithmetic and copies ran while one was open for 17% of the time, Pallas kernels for 0%

commit v1 on v0

--- a/solution.py
+++ b/solution.py
@@ -163,7 +163,9 @@
     cross_part = jnp.einsum(
         "hrc,che->rhe", cross_low, vc_heads, preferred_element_type=jnp.float32
     ).reshape(full_rows, model_width)
-    crossed = lax.psum(cross_part, "mem")
+    crossed = cross_part
+    for hop in (1, 2):
+        crossed = crossed + lax.ppermute(crossed, "mem", [(dev, dev ^ hop) for dev in range(4)])
     crossed_low = crossed.astype(jnp.bfloat16)
     second, second_norm, second_inv = normalize(
         first_out + product(crossed_low, cross_out) + proj_bias[5], norm_gain[1], norm_shift[1]

time: 1820 us -> 1840 us (1.011)
  waiting for transfers between devices: 1030 us -> 1120 us
  blocking collectives: 139 us -> 61 us
    ppermute x0 -> x2, waiting for transfers between devices: none -> 94.5 us  [per_device(): lax.ppermute(crossed, 'mem', [(dev, dev ^ hop) for dev in range(4)])]
    psum x1 -> x0, blocking collectives: 77.8 us -> none  [per_device(): crossed = lax.psum(cross_part, 'mem')]
  transfers between devices with their start and end apart: 10 -> 12, of which waited for: 8 -> 10; matrix products, arithmetic and copies ran while one was open for 17% -> 17% of each run, Pallas kernels for 0% -> 0%
where the time goes in v1:
time: 1840 us; the launch traced here: 1830 us
  waiting for transfers between devices  1120 us (61%)
  matrix products  454 us (25%)
  other arithmetic  112 us (6%)
  blocking collectives  61 us (3%)
  local copies, waits for them, and re-layouts  60.3 us (3%)
    reduce_scatter x1, waiting for transfers between devices, per_device(): lax.psum_scatter(ffn_in_grad, 'dp', scatter_dimension=0, tiled=True)  284 us
    reduce_scatter x1, waiting for transfers between devices, per_device(): lax.psum_scatter(ffn_out_grad, 'dp', scatter_dimension=0, tiled=True)  284 us
    ppermute x2, waiting for transfers between devices, per_device(): lax.ppermute(crossed, 'mem', [(dev, dev ^ hop) for dev in range(4)])  94.5 us
    reduce_scatter x1, waiting for transfers between devices, per_device(): lax.psum_scatter(cross_q_grad, 'dp', scatter_dimension=0, tiled=True)  92.2 us
    reduce_scatter x1, waiting for transfers between devices, per_device(): lax.psum_scatter(self_out_grad, 'dp', scatter_dimension=0, tiled=True)  92.2 us
    reduce_scatter x1, waiting for transfers between devices, per_device(): lax.psum_scatter(qkv_weight_grad, 'dp', scatter_dimension=0, tiled=True)  91.6 us
    dot_general x7, matrix products, product(): return jnp.dot(left_rows, right_rows, preferred_element_type=jnp.float32)  90.6 us
    reduce_scatter x1, waiting for transfers between devices, per_device(): lax.psum_scatter(cross_out_grad, 'dp', scatter_dimension=0, tiled=True)  88.5 us
  transfers between devices with their start and end apart: 12, of which 10 were waited for; matrix products, arithmetic and copies ran while one was open for 17% of the time, Pallas kernels for 0%

profile of v1, /device:TPU:0, one launch (start us, length us, event | category | flops | bytes accessed | tf_op | source)
XLA Modules:
  0.0 1831.1 jit_solution(13103761637117372332)
XLA Ops:
  23.3 12.1 fusion.78
  53.7 35.8 %fusion.79 = (f32[16,1024]{1,0:T(8,128)S(1)}, f32[16,1024,1024]{1,2,0:T(8,128)}) fusion(pred[1024,1024]{0,1:T(8,128)(4,1)S(1)} %fusion.35, bf16[1024,16,64]{0,2,1:T(8,128)(2,1)} %bitcast.167, bf16[1024,16,64]{0,2,1:T(8,128)(2,1)} %bitcast.172), kind=kOutput, calls=%fused_computation.155 | convolution fusion | flops 2214593536 | bytes 72417280 | tf_op jit(solution)/shard_map/sub | solution.py:63
  89.6 24.3 %fusion.42 = bf16[16,64,1024]{2,1,0:T(8,128)(2,1)} fusion(bf16[1024,16,64]{0,2,1:T(8,128)(2,1)} %bitcast.182, f32[16,1024,1024]{1,2,0:T(8,128)} %get-tuple-element.239, f32[16,1024]{1,0:T(8,128)S(1)} %get-tuple-element.238), kind=kOutput, calls=%fused_computation.104 | convolution fusion | flops 2182086656 | bytes 71368704 | tf_op jit(solution)/shard_map/hrc,che->rhe/dot_general | solution.py:127
  113.9 4.3 fusion.80
  128.2 8.9 select_reduce_fusion.2
  137.0 7.2 all-gather
  144.3 9.6 select_reduce_fusion.1
  153.8 6.1 all-gather.1
  160.2 8.1 fusion.33
  168.7 6.8 collective-permute-done
  184.0 87.7 %collective-permute-done.1 = f32[1024,1024]{0,1:T(8,128)} collective-permute-done((f32[1024,1024]{0,1:T(8,128)}, f32[1024,1024]{0,1:T(8,128)}, u32[]{:S(2)}, u32[]{:S(2)}) %collective-permute-start.1) | collective-permute-done | bytes 4194336 | tf_op jit(solution)/shard_map/ppermute | solution.py:168
  271.6 4.3 add_convert_fusion.2
  281.4 46.4 %multiply_convert_fusion.2 = (bf16[1024,4096]{1,0:T(8,128)(2,1)}, f32[1024,4096]{1,0:T(8,128)}, f32[1024,4096]{1,0:T(8,128)}) fusion(f32[4096]{0:T(1024)S(1)} %copy-done.79, bf16[1024,4096]{1,0:T(8,128)(2,1)S(1)} %bitcast.233, bf16[1024,1024]{0,1:T(8,128)(2,1)S(1)} %fusion.67.clone.4), kind=kOutput, calls=%fused_computation.20 | convolution fusion | flops 8866758656 | bytes 52445184 | tf_op jit(solution)/shard_map/dot_general | solution.py:23
  327.8 16.9 fusion.82
  355.3 24.5 %convert_reduce_fusion = (f32[4096]{0:T(1024)}, bf16[1024,4096]{1,0:T(8,128)(2,1)}) fusion(f32[1024,4096]{1,0:T(8,128)} %get-tuple-element.215, f32[1024,4096]{1,0:T(8,128)} %get-tuple-element.246, f32[4096]{0:T(1024)S(1)} %copy-done.79, bf16[1024,1024]{0,1:T(8,128)(2,1)} %get-tuple-element.209, bf16[4096,1024]{1,0:T(8,128)(2,1)} %param.29), kind=kOutput, calls=%fused_computation.16 | convolution fusion | flops 8661233664 | bytes 52461568 | tf_op jit(solution)/shard_map/dot_general | solution.py:33
  379.8 18.5 %multiply_reduce_fusion.2 = (f32[1024]{0:T(1024)}, f32[1024]{0:T(1024)S(1)}, f32[1024]{0:T(1024)S(1)}, f32[1024]{0:T(1024)}, f32[1024,1024]{0,1:T(8,128)S(1)}) fusion(f32[1024,1024]{0,1:T(8,128)S(1)} %copy-done.4, f32[1024]{0:T(1024)S(1)} %add_rsqrt_fusion.1, f32[1024]{0:T(1024)S(1)} %broadcast_multiply_fusion.7, f32[1024]{0:T(1024)S(1)} %bitcast.195, ...), kind=kOutput, calls=%fused_computation.60 | convolution fusion | flops 8609853440 | bytes 31507456 | tf_op jit(solution)/shard_map/dot_general | solution.py:33
  402.8 14.6 multiply_reduce_fusion.1
  417.4 32.9 %all-reduce.7.cloned.1.call-done = f32[16,1024]{1,0:T(8,128)} async-done(((f32[16,1024]{1,0:T(8,128)}), f32[16,1024]{1,0:T(8,128)}) %all-reduce.7.cloned.1.call-update) | async-done | bytes 65552 | tf_op jit(solution)/shard_map/psum | solution.py:196
  450.3 12.4 multiply_convert_fusion.1
  467.1 5.4 copy.76
  472.6 9.6 fusion.48
  482.3 6.3 convolution_convert_fusion.3
  489.4 4.5 convolution_bitcast_fusion.1
  493.9 64.2 %all-reduce.9.cloned.1.call-done = f32[1024,1024]{1,0:T(8,128)} async-done(((f32[1024,1024]{1,0:T(8,128)}), f32[1024,1024]{1,0:T(8,128)}) %all-reduce.9.cloned.1.call-update) | async-done | bytes 4194320 | tf_op jit(solution)/shard_map/psum | solution.py:201
  558.2 8.5 multiply_reduce_fusion.3
  571.9 43.5 %multiply_reduce_fusion = (f32[16,1024]{1,0:T(8,128)S(1)}, f32[16,1024,1024]{1,2,0:T(8,128)}) fusion(f32[16,1024,1024]{1,2,0:T(8,128)} %get-tuple-element.239, f32[16,1024]{1,0:T(8,128)S(1)} %copy-done.35, bf16[1024,16,64]{0,2,1:T(8,128)(2,1)S(1)} %bitcast.238, bf16[1024,16,64]{0,2,1:T(8,128)(2,1)S(1)} %bitcast.183), kind=kOutput, calls=%fused_computation.7 | convolution fusion | flops 2197798912 | bytes 138543104 | tf_op jit(solution)/shard_map/rhe,che->hrc/dot_general | solution.py:222
  615.4 54.7 %multiply_convert_fusion = bf16[16,1024,1024]{1,2,0:T(8,128)(2,1)} fusion(f32[16,1024,1024]{1,2,0:T(8,128)} %get-tuple-element.254, f32[16,1024]{1,0:T(8,128)S(1)} %get-tuple-element.253, f32[16,1024,1024]{1,2,0:T(8,128)} %get-tuple-element.239, f32[16,1024]{1,0:T(8,128)S(1)} %copy-done.35), kind=kLoop, calls=%fused_computation.6 | loop fusion | flops 67108864 | bytes 167903232 | tf_op jit(solution)/shard_map/convert_element_type | solution.py:225
  670.1 17.3 convolution_convert_fusion
  687.5 18.8 %multiply_convert_fusion.3 = bf16[16,64,1024]{2,1,0:T(8,128)(2,1)} fusion(bf16[1024,16,64]{0,2,1:T(8,128)(2,1)} %bitcast.173, bf16[16,1024,1024]{1,2,0:T(8,128)(2,1)} %multiply_convert_fusion), kind=kOutput, calls=%fused_computation.67 | convolution fusion | flops 2149580800 | bytes 37748736 | tf_op jit(solution)/shard_map/hrc,che->rhe/dot_general | solution.py:227
  706.2 25.3 %fusion.45 = bf16[16,64,1024]{2,1,0:T(8,128)(2,1)} fusion(bf16[1024,16,64]{0,2,1:T(8,128)(2,1)} %bitcast.239, f32[16,1024,1024]{1,2,0:T(8,128)} %get-tuple-element.239, f32[16,1024]{1,0:T(8,128)S(1)} %copy-done.35), kind=kOutput, calls=%fused_computation.105 | convolution fusion | flops 2182086656 | bytes 71368704 | tf_op jit(solution)/shard_map/hrc,rhe->che/dot_general | solution.py:216
  733.7 13.6 convolution_bitcast_fusion
  747.6 7.3 fusion.59
  755.7 7.9 fusion.63
  763.7 7.1 fusion.56
  771.5 16.6 fusion.64
  788.5 16.3 fusion.84
  810.0 4.6 convolution_bitcast_fusion.2
  814.7 4.6 convert_reduce_fusion.1
  819.9 41.6 %all-reduce.12 = (f32[6,1024]{1,0:T(8,128)S(1)}, bf16[1024]{0:T(1024)(128)(2,1)S(1)}, f32[4096]{0:T(1024)}, f32[3,1024]{1,0:T(4,128)}, f32[3,1024]{1,0:T(4,128)}) all-reduce(f32[6,1024]{1,0:T(8,128)S(1)} %stack.51, f32[1024]{0:T(1024)S(1)} %convert_reduce_fusion.6, f32[4096]{0:T(1024)S(1)} %copy-done.60, ...), channel_id=1, replica_groups=mesh['dp'=8,'mem'=4] {'dp'}, use_global_device_ids=true, to_apply=%region_35.36 | all-reduce | flops 17408 | bytes 137216 | tf_op jit(solution)/shard_map/psum | solution.py:271
  861.5 12.4 add_bitcast_fusion
  874.0 5.5 copy.85
  879.5 6.1 psum.68
  888.4 91.6 %reduce-scatter.8.cloned.1.call-done = f32[128,3072]{0,1:T(8,128)} async-done(((f32[1024,3072]{0,1:T(8,128)}), f32[128,3072]{0,1:T(8,128)}) %reduce-scatter.8.cloned.1.call-update) | async-done | bytes 1572880 | tf_op jit(solution)/shard_map/reduce_scatter | solution.py:263
  983.0 88.5 %reduce-scatter.16.cloned.1.call-done = f32[128,1024]{1,0:T(8,128)} async-done(((f32[1024,1024]{1,0:T(8,128)}), f32[128,1024]{1,0:T(8,128)}) %reduce-scatter.16.cloned.1.call-update) | async-done | bytes 524304 | tf_op jit(solution)/shard_map/reduce_scatter | solution.py:267
  1071.5 92.2 %reduce-scatter.12.cloned.1.call-done = f32[128,1024]{1,0:T(8,128)} async-done(((f32[1024,1024]{1,0:T(8,128)}), f32[128,1024]{1,0:T(8,128)}) %reduce-scatter.12.cloned.1.call-update) | async-done | bytes 524304 | tf_op jit(solution)/shard_map/reduce_scatter | solution.py:265
  1163.6 92.2 %reduce-scatter.10.cloned.1.call-done = f32[128,1024]{1,0:T(8,128)} async-done(((f32[1024,1024]{1,0:T(8,128)}), f32[128,1024]{1,0:T(8,128)}) %reduce-scatter.10.cloned.1.call-update) | async-done | bytes 524304 | tf_op jit(solution)/shard_map/reduce_scatter | solution.py:264
  1255.8 284.3 %reduce-scatter.18.cloned.1.call-done = f32[128,4096]{1,0:T(8,128)} async-done(((f32[1024,4096]{1,0:T(8,128)}), f32[128,4096]{1,0:T(8,128)}) %reduce-scatter.18.cloned.1.call-update) | async-done | bytes 2097168 | tf_op jit(solution)/shard_map/reduce_scatter | solution.py:268
  1540.2 283.6 %reduce-scatter.20.cloned.1.call-done = f32[512,1024]{1,0:T(8,128)} async-done(((f32[4096,1024]{1,0:T(8,128)}), f32[512,1024]{1,0:T(8,128)}) %reduce-scatter.20.cloned.1.call-update) | async-done | bytes 2097168 | tf_op jit(solution)/shard_map/reduce_scatter | solution.py:269
  (260 shorter events, 98.9 us)
Async XLA Ops:
  7.2 112.9 %copy-start = (bf16[1024,1024]{1,0:T(8,128)(2,1)S(1)}, bf16[1024,1024]{1,0:T(8,128)(2,1)}, u32[]{:S(2)}) copy-start(bf16[1024,1024]{1,0:T(8,128)(2,1)} %param.25) | copy-start | bytes 6291460
  7.2 443.1 %all-reduce.7.cloned.1.call-start = ((), (), s32[]{:S(2)}) async-start(), calls=%async_computation.7 | async-start | bytes 131072 | tf_op jit(solution)/shard_map/psum | solution.py:196
  8.7 10.3 copy-start.61
  89.6 24.3 %copy-start.34 = (f32[16,1024]{1,0:T(8,128)}, f32[16,1024]{1,0:T(8,128)S(1)}, u32[]{:S(2)}) copy-start(f32[16,1024]{1,0:T(8,128)S(1)} %get-tuple-element.238) | copy-start | bytes 196612
  89.6 24.3 %copy-start.28 = (bf16[1,1024,1024]{1,2,0:T(8,128)(2,1)S(1)}, bf16[1,1024,1024]{1,2,0:T(8,128)(2,1)}, u32[]{:S(2)}) copy-start(bf16[1,1024,1024]{1,2,0:T(8,128)(2,1)} %copy.62) | copy-start | bytes 6291460
  89.6 24.3 %copy-start.68 = (f32[1,1024]{1,0:T(1,128)S(1)}, f32[1,1024]{1,0:T(1,128)}, u32[]{:S(2)}) copy-start(f32[1,1024]{1,0:T(1,128)} %get-tuple-element.224) | copy-start | bytes 12292
  89.6 24.3 %copy-start.77 = (bf16[1024,1024]{1,0:T(8,128)(2,1)S(1)}, bf16[1024,1024]{1,0:T(8,128)(2,1)}, u32[]{:S(2)}) copy-start(bf16[1024,1024]{1,0:T(8,128)(2,1)} %param.24) | copy-start | bytes 6291460
  118.2 157.7 %copy-start.43 = (f32[1024]{0:T(1024)}, f32[1024]{0:T(1024)S(1)}, u32[]{:S(2)}) copy-start(f32[1024]{0:T(1024)S(1)} %broadcast_multiply_fusion.8) | copy-start | bytes 12292
  118.7 157.3 %copy-start.51 = (f32[1024]{0:T(1024)}, f32[1024]{0:T(1024)S(1)}, u32[]{:S(2)}) copy-start(f32[1024]{0:T(1024)S(1)} %add_rsqrt_fusion.2) | copy-start | bytes 12292
  128.2 32.0 %copy-start.63 = (pred[256]{0:T(512)(128)(4,1)}, pred[256]{0:T(512)(128)(4,1)S(1)}, u32[]{:S(2)}) copy-start(pred[256]{0:T(512)(128)(4,1)S(1)} %add_compare_fusion) | copy-start | bytes 772
  144.3 15.9 copy-start.32
  160.1 8.1 copy-start.19
  160.2 8.1 copy-start.21
  168.3 7.2 collective-permute-start
  178.5 93.1 %collective-permute-start.1 = (f32[1024,1024]{0,1:T(8,128)}, f32[1024,1024]{0,1:T(8,128)}, u32[]{:S(2)}, u32[]{:S(2)}) collective-permute-start(f32[1024,1024]{0,1:T(8,128)} %bitcast_add_fusion), channel_id=1, source_target_pairs={{0,2},{1,3},{2,0},{3,1},{4,6},{5,7},{6,4},{7,5},{8,10},{9,11},{10,... | collective-permute-start | bytes 12582920 | tf_op jit(solution)/shard_map/ppermute | solution.py:168
  184.0 92.0 %copy-start.9 = (f32[1024,1024]{0,1:T(8,128)S(1)}, f32[1024,1024]{0,1:T(8,128)}, u32[]{:S(2)}) copy-start(f32[1024,1024]{0,1:T(8,128)} %copy-done.8) | copy-start | bytes 12582916
  184.0 92.0 %copy-start.66 = (f32[1,1024]{1,0:T(1,128)S(1)}, f32[1,1024]{1,0:T(1,128)}, u32[]{:S(2)}) copy-start(f32[1,1024]{1,0:T(1,128)} %get-tuple-element.227) | copy-start | bytes 12292
  184.0 92.1 %copy-start.75 = (bf16[1024,1024]{1,0:T(8,128)(2,1)S(1)}, bf16[1024,1024]{1,0:T(8,128)(2,1)}, u32[]{:S(2)}) copy-start(bf16[1024,1024]{1,0:T(8,128)(2,1)} %param.27) | copy-start | bytes 6291460
  271.6 9.8 slice-start
  276.0 5.4 slice-start.1
  279.4 118.8 %copy-start.36 = (f32[1024]{0:T(1024)}, f32[1024]{0:T(1024)S(1)}, u32[]{:S(2)}) copy-start(f32[1024]{0:T(1024)S(1)} %broadcast_multiply_fusion.7) | copy-start | bytes 12292
  279.9 118.3 %copy-start.38 = (f32[1024]{0:T(1024)}, f32[1024]{0:T(1024)S(1)}, u32[]{:S(2)}) copy-start(f32[1024]{0:T(1024)S(1)} %add_rsqrt_fusion.1) | copy-start | bytes 12292
  281.4 46.4 %copy-start.65 = (f32[1,1024]{1,0:T(1,128)S(1)}, f32[1,1024]{1,0:T(1,128)}, u32[]{:S(2)}) copy-start(f32[1,1024]{1,0:T(1,128)} %get-tuple-element.221) | copy-start | bytes 12292
  327.8 19.7 %copy-start.6 = (bf16[1,1024,1024]{1,2,0:T(8,128)(2,1)S(1)}, bf16[1,1024,1024]{1,2,0:T(8,128)(2,1)}, u32[]{:S(2)}) copy-start(bf16[1,1024,1024]{1,2,0:T(8,128)(2,1)} %copy.73) | copy-start | bytes 6291460
  355.3 24.5 %copy-start.4 = (f32[1024,1024]{0,1:T(8,128)S(1)}, f32[1024,1024]{0,1:T(8,128)}, u32[]{:S(2)}) copy-start(f32[1024,1024]{0,1:T(8,128)} %copy-done.3) | copy-start | bytes 12582916
  402.7 14.6 copy-start.80
  417.4 140.8 %all-reduce.9.cloned.1.call-start = ((), (), s32[]{:S(2)}) async-start(), calls=%async_computation.8 | async-start | bytes 8388608 | tf_op jit(solution)/shard_map/psum | solution.py:201
  450.3 12.4 copy-start.15
  472.5 259.0 %reduce-scatter.14.cloned.1.call-start = ((), (), s32[]{:S(2)}) async-start(), calls=%async_computation.12 | async-start | bytes 9437184 | tf_op jit(solution)/shard_map/reduce_scatter | solution.py:266
  472.6 9.6 copy-start.7
  482.2 6.4 copy-start.24
  482.2 7.1 copy-start.31
  493.9 64.3 %copy-start.44 = (f32[1024]{0:T(1024)S(1)}, f32[1024]{0:T(1024)}, u32[]{:S(2)}) copy-start(f32[1024]{0:T(1024)} %copy-done.43) | copy-start | bytes 12292
  493.9 64.3 %copy-start.52 = (f32[1024]{0:T(1024)S(1)}, f32[1024]{0:T(1024)}, u32[]{:S(2)}) copy-start(f32[1024]{0:T(1024)} %copy-done.51) | copy-start | bytes 12292
  493.9 64.3 %copy-start.57 = (f32[1,1024]{1,0:T(1,128)S(1)}, f32[1,1024]{1,0:T(1,128)}, u32[]{:S(2)}) copy-start(f32[1,1024]{1,0:T(1,128)} %get-tuple-element.229) | copy-start | bytes 12292
  493.9 392.3 %all-reduce.11.cloned.1.call-start = ((), (), s32[]{:S(2)}) async-start(), calls=%async_computation.13 | async-start | bytes 1048576 | tf_op jit(solution)/shard_map/psum | solution.py:273
  558.2 8.5 copy-start.10
  571.1 44.3 %copy-start.81 = (bf16[1024,1024]{0,1:T(8,128)(2,1)}, bf16[1024,1024]{0,1:T(8,128)(2,1)S(1)}, u32[]{:S(2)}) copy-start(bf16[1024,1024]{0,1:T(8,128)(2,1)S(1)} %convolution_convert_fusion.1) | copy-start | bytes 6291460
  615.4 54.7 %copy-start.11 = (bf16[1024,1024]{0,1:T(8,128)(2,1)S(1)}, bf16[1024,1024]{0,1:T(8,128)(2,1)}, u32[]{:S(2)}) copy-start(bf16[1024,1024]{0,1:T(8,128)(2,1)} %copy.64) | copy-start | bytes 6291460
  706.2 27.5 %copy-start.12 = (bf16[16,64,1024]{2,1,0:T(8,128)(2,1)S(1)}, bf16[16,64,1024]{2,1,0:T(8,128)(2,1)}, u32[]{:S(2)}) copy-start(bf16[16,64,1024]{2,1,0:T(8,128)(2,1)} %convolution_convert_fusion) | copy-start | bytes 6291460
  733.7 246.3 %reduce-scatter.8.cloned.1.call-start = ((), (), s32[]{:S(2)}) async-start(), calls=%async_computation.9 | async-start | bytes 14155776 | tf_op jit(solution)/shard_map/reduce_scatter | solution.py:263
  747.4 324.1 %reduce-scatter.16.cloned.1.call-start = ((), (), s32[]{:S(2)}) async-start(), calls=%async_computation.14 | async-start | bytes 4718592 | tf_op jit(solution)/shard_map/reduce_scatter | solution.py:267
  755.0 408.7 %reduce-scatter.12.cloned.1.call-start = ((), (), s32[]{:S(2)}) async-start(), calls=%async_computation.11 | async-start | bytes 4718592 | tf_op jit(solution)/shard_map/reduce_scatter | solution.py:265
  763.6 492.2 %reduce-scatter.10.cloned.1.call-start = ((), (), s32[]{:S(2)}) async-start(), calls=%async_computation.10 | async-start | bytes 4718592 | tf_op jit(solution)/shard_map/reduce_scatter | solution.py:264
  770.9 769.3 %reduce-scatter.18.cloned.1.call-start = ((), (), s32[]{:S(2)}) async-start(), calls=%async_computation.15 | async-start | bytes 18874368 | tf_op jit(solution)/shard_map/reduce_scatter | solution.py:268
  788.2 1035.6 %reduce-scatter.20.cloned.1.call-start = ((), (), s32[]{:S(2)}) async-start(), calls=%async_computation.16 | async-start | bytes 18874368 | tf_op jit(solution)/shard_map/reduce_scatter | solution.py:269
  814.7 5.1 copy-start.60
  874.0 949.8 %copy-start.1 = (bf16[1024,1024]{1,0:T(8,128)(2,1)S(1)}, bf16[1024,1024]{1,0:T(8,128)(2,1)}, u32[]{:S(2)}) copy-start(bf16[1024,1024]{1,0:T(8,128)(2,1)} %param.25) | copy-start | bytes 6291460
  (48 other events, 134.6 us)
Sparse Core Ops, SparseCore 0:
  417.5 32.7 all-reduce.6
  472.7 85.4 all-reduce.8
  561.8 147.9 reduce-scatter.13
  733.8 33.1 all-reduce.10
  770.5 209.4 reduce-scatter.7
  984.0 87.3 reduce-scatter.15
  1075.7 87.9 reduce-scatter.11
  1167.8 87.9 reduce-scatter.9
  1260.2 279.9 reduce-scatter.17
  1544.4 279.3 reduce-scatter.19
